TPU v7x, 32 devices: a whole 2x2x4 slice. The times are simulated.
32 devices in a mesh: real: 2 (over x), tile: 16 (over z, y, core).
Axes of the slice: x: 2, y: 2, z: 4, core: 2. Of those that a mesh axis runs over, the one named last changes fastest.
Arguments:
- positions: float32 [6, 8192], P('real', 'tile'), parts along dimension 0, may hold values from -1.5 to 125.5, as said below
- residual: float32 [6, 8192], P('real', 'tile'), parts along dimension 0, may hold values from -24 to 24
- iterate: float32 [6, 8192], P('real', 'tile'), parts along dimension 0, may hold values from -6 to 6
Outputs:
- new_iterate: float32 [6, 8192], P('real', 'tile'), parts along dimension 0
- new_residual: float32 [6, 8192], P('real', 'tile'), parts along dimension 0
- new_direction: float32 [6, 8192], P('real', 'tile'), parts along dimension 0
There are 2 independent parts, one for each index of `real`. A program takes and returns all parts, laid end to end along the dimension named above; each array names one. Nothing has to cross between parts.
Inputs may be any that keep to these rules, and one draw needn't show every extreme that they name: `positions`: distinct blobs are at least 1 apart.
All inputs are finite; a program needn't handle non-finite values.
Results may differ from a plain program's by a relative error of at most 0.0003.
Values sent between devices are 32-bit elements; how exact they have to be, the bound alone decides.
A program may use at most 64 MiB of HBM per device.

v0:
```python
import jax
import jax.numpy as jnp
from jax import lax
from jax.sharding import PartitionSpec as P


def pair_terms(row_pos, col_pos):
    separation = row_pos[:, :, None] - col_pos[:, None, :]
    squared = jnp.sum(separation * separation, axis=0)
    radius = jnp.sqrt(squared)
    inverse = 1.0 / jnp.maximum(radius, 0.5)
    inverse_sq = inverse * inverse
    far_scalar = 0.75 * inverse * (1.0 + 2.0 / 3.0 * inverse_sq)
    far_tensor = 0.75 * (1.0 - 2.0 * inverse_sq) * inverse_sq * inverse
    touching = radius < 2.0
    scalar_part = jnp.where(touching, 1.0 - 9.0 / 32.0 * radius, far_scalar)
    tensor_part = jnp.where(touching, 3.0 / 32.0 * inverse, far_tensor)
    return (separation, scalar_part, tensor_part)


def toward_rows(separation, scalar_part, tensor_part, col_forces):
    projected = jnp.sum(separation * col_forces[:, None, :], axis=0)
    return jnp.sum(
        scalar_part[None] * col_forces[:, None, :] + (tensor_part * projected)[None] * separation,
        axis=2,
    )


def shards(positions, residual, iterate):
    own_blobs = positions.shape[1]
    old_norm = lax.psum(jnp.sum(residual * residual), "tile")
    col_pos = lax.all_gather(positions, "tile", axis=1, tiled=True)
    col_forces = lax.all_gather(residual, "tile", axis=1, tiled=True)
    portion_cols = col_pos.shape[1]
    col_block = portion_cols
    for factor in (4, 2, 1):
        col_block = factor * own_blobs
        break

    def add_block(turn_index, running):
        block_pos = lax.dynamic_slice_in_dim(col_pos, turn_index * col_block, col_block, 1)
        block_forces = lax.dynamic_slice_in_dim(col_forces, turn_index * col_block, col_block, 1)
        separation, scalar_part, tensor_part = pair_terms(positions, block_pos)
        return running + toward_rows(separation, scalar_part, tensor_part, block_forces)

    applied = lax.fori_loop(0, portion_cols // col_block, add_block, jnp.zeros_like(residual))
    curvature = lax.psum(jnp.sum(residual * applied), "tile")
    step_size = old_norm / curvature
    new_residual = residual - step_size * applied
    new_norm = lax.psum(jnp.sum(new_residual * new_residual), "tile")
    new_iterate = iterate + step_size * residual
    new_direction = new_residual + new_norm / old_norm * residual
    return (new_iterate, new_residual, new_direction)


def solution(mesh):
    return jax.shard_map(
        shards,
        mesh=mesh,
        in_specs=(P("real", "tile"), P("real", "tile"), P("real", "tile")),
        out_specs=(P("real", "tile"), P("real", "tile"), P("real", "tile")),
        check_vma=False,
    )
```

profile of v0, /device:TPU:0, one launch (start us, length us, event | category | flops | bytes accessed | tf_op | source)
XLA Modules:
  0.0 165.1 jit_solution(6442482215898881509)
XLA Ops:
  0.6 23.7 %all_gather.6 = f32[3,8192]{1,0:T(4,128)S(1)} all-gather(f32[3,512]{1,0:T(4,128)} %param.5), channel_id=1, replica_groups=mesh['real'=2,'tile'=16] {'tile'}, dimensions={1}, use_global_device_ids=true | all-gather | bytes 104448 | tf_op jit(solution)/shard_map/all_gather | solution.py:32
  24.3 18.0 %all_gather.7 = f32[3,8192]{1,0:T(4,128)S(1)} all-gather(f32[3,512]{1,0:T(4,128)} %param.6), channel_id=1, replica_groups=mesh['real'=2,'tile'=16] {'tile'}, dimensions={1}, use_global_device_ids=true | all-gather | bytes 104448 | tf_op jit(solution)/shard_map/all_gather | solution.py:33
  42.4 0.0 copy-start.1
  42.4 0.0 copy-start.3
  42.4 56.4 %while.14 = (s32[]{:T(128)}, f32[3,512]{1,0:T(4,128)S(1)}, f32[3,512]{1,0:T(4,128)}, f32[3,8192]{1,0:T(4,128)S(1)}, f32[3,8192]{1,0:T(4,128)S(1)}, /*index=5*/s32[]{:T(128)}, s32[]{:T(128)}, s32[]{:T(128)}, s32[]{:T(128)}) while((s32[]{:T(128)}, f32[3,512]{1,0:T(4,128)S(1)}, f32[3,512]{1,0:T(4,128)}, f32[3,8192]{1,0:T(4,128)S(1)}, ...), condition=%wide.region_6.7_spmd.clone, body=%wide.region_2.6_spmd.clone.sunk | while | flops 49284612 | bytes 33812656 | solution.py:46
  42.4 8.2 %fusion.10 = (f32[512,2048]{1,0:T(8,128)S(1)}, f32[512,2048]{1,0:T(8,128)S(1)}) fusion(f32[3,2048]{1,0:T(4,128)S(1)} %get-tuple-element.177, f32[3,512]{1,0:T(4,128)} %get-tuple-element.203, f32[3,2048]{1,0:T(4,128)S(1)} %get-tuple-element.178), kind=kLoop, calls=%fused_computation.3.clone.1 | loop fusion | flops 13631488 | bytes 8443904 | tf_op jit(solution)/shard_map/while/body/eval_jaxpr/reduce_sum | solution.py:9
  50.6 0.0 copy-start
  50.6 3.6 %fusion.11 = (f32[512,2048]{1,0:T(8,128)S(1)}, f32[512,2048]{1,0:T(8,128)S(1)}) fusion(f32[512,2048]{1,0:T(8,128)S(1)} %get-tuple-element.179, f32[512,2048]{1,0:T(8,128)S(1)} %get-tuple-element.180), kind=kLoop, calls=%fused_computation.11.clone.1 | loop fusion | flops 19922944 | bytes 16777216 | tf_op jit(solution)/shard_map/while/body/eval_jaxpr/jit(_where)/select_n | solution.py:16
  54.2 0.0 copy-done
  54.2 2.3 %fusion.12 = f32[3,512]{1,0:T(4,128)S(1)} fusion(f32[512,2048]{1,0:T(8,128)S(1)} %get-tuple-element.181, f32[3,2048]{1,0:T(4,128)S(1)} %get-tuple-element.178, f32[512,2048]{1,0:T(8,128)S(1)} %get-tuple-element.182, f32[3,2048]{1,0:T(4,128)S(1)} %get-tuple-element.177, f32[3,512]{1,0:T(4,128)S(1)} %copy-done), kind=kLoop, calls=%fused_computation.6.clone.1 | loop fusion | flops 15727104 | bytes 8450048 | tf_op jit(solution)/shard_map/while/body/eval_jaxpr/reduce_sum | solution.py:23
  56.5 8.2 %fusion.10 = (f32[512,2048]{1,0:T(8,128)S(1)}, f32[512,2048]{1,0:T(8,128)S(1)}) fusion(f32[3,2048]{1,0:T(4,128)S(1)} %get-tuple-element.177, f32[3,512]{1,0:T(4,128)} %get-tuple-element.203, f32[3,2048]{1,0:T(4,128)S(1)} %get-tuple-element.178), kind=kLoop, calls=%fused_computation.3.clone.1 | loop fusion | flops 13631488 | bytes 8443904 | tf_op jit(solution)/shard_map/while/body/eval_jaxpr/reduce_sum | solution.py:9
  64.7 0.0 copy-start
  64.7 3.6 %fusion.11 = (f32[512,2048]{1,0:T(8,128)S(1)}, f32[512,2048]{1,0:T(8,128)S(1)}) fusion(f32[512,2048]{1,0:T(8,128)S(1)} %get-tuple-element.179, f32[512,2048]{1,0:T(8,128)S(1)} %get-tuple-element.180), kind=kLoop, calls=%fused_computation.11.clone.1 | loop fusion | flops 19922944 | bytes 16777216 | tf_op jit(solution)/shard_map/while/body/eval_jaxpr/jit(_where)/select_n | solution.py:16
  68.3 0.0 copy-done
  68.3 2.3 %fusion.12 = f32[3,512]{1,0:T(4,128)S(1)} fusion(f32[512,2048]{1,0:T(8,128)S(1)} %get-tuple-element.181, f32[3,2048]{1,0:T(4,128)S(1)} %get-tuple-element.178, f32[512,2048]{1,0:T(8,128)S(1)} %get-tuple-element.182, f32[3,2048]{1,0:T(4,128)S(1)} %get-tuple-element.177, f32[3,512]{1,0:T(4,128)S(1)} %copy-done), kind=kLoop, calls=%fused_computation.6.clone.1 | loop fusion | flops 15727104 | bytes 8450048 | tf_op jit(solution)/shard_map/while/body/eval_jaxpr/reduce_sum | solution.py:23
  70.6 8.2 %fusion.10 = (f32[512,2048]{1,0:T(8,128)S(1)}, f32[512,2048]{1,0:T(8,128)S(1)}) fusion(f32[3,2048]{1,0:T(4,128)S(1)} %get-tuple-element.177, f32[3,512]{1,0:T(4,128)} %get-tuple-element.203, f32[3,2048]{1,0:T(4,128)S(1)} %get-tuple-element.178), kind=kLoop, calls=%fused_computation.3.clone.1 | loop fusion | flops 13631488 | bytes 8443904 | tf_op jit(solution)/shard_map/while/body/eval_jaxpr/reduce_sum | solution.py:9
  78.8 0.0 copy-start
  78.8 3.6 %fusion.11 = (f32[512,2048]{1,0:T(8,128)S(1)}, f32[512,2048]{1,0:T(8,128)S(1)}) fusion(f32[512,2048]{1,0:T(8,128)S(1)} %get-tuple-element.179, f32[512,2048]{1,0:T(8,128)S(1)} %get-tuple-element.180), kind=kLoop, calls=%fused_computation.11.clone.1 | loop fusion | flops 19922944 | bytes 16777216 | tf_op jit(solution)/shard_map/while/body/eval_jaxpr/jit(_where)/select_n | solution.py:16
  82.4 0.0 copy-done
  82.4 2.3 %fusion.12 = f32[3,512]{1,0:T(4,128)S(1)} fusion(f32[512,2048]{1,0:T(8,128)S(1)} %get-tuple-element.181, f32[3,2048]{1,0:T(4,128)S(1)} %get-tuple-element.178, f32[512,2048]{1,0:T(8,128)S(1)} %get-tuple-element.182, f32[3,2048]{1,0:T(4,128)S(1)} %get-tuple-element.177, f32[3,512]{1,0:T(4,128)S(1)} %copy-done), kind=kLoop, calls=%fused_computation.6.clone.1 | loop fusion | flops 15727104 | bytes 8450048 | tf_op jit(solution)/shard_map/while/body/eval_jaxpr/reduce_sum | solution.py:23
  84.7 8.2 %fusion.10 = (f32[512,2048]{1,0:T(8,128)S(1)}, f32[512,2048]{1,0:T(8,128)S(1)}) fusion(f32[3,2048]{1,0:T(4,128)S(1)} %get-tuple-element.177, f32[3,512]{1,0:T(4,128)} %get-tuple-element.203, f32[3,2048]{1,0:T(4,128)S(1)} %get-tuple-element.178), kind=kLoop, calls=%fused_computation.3.clone.1 | loop fusion | flops 13631488 | bytes 8443904 | tf_op jit(solution)/shard_map/while/body/eval_jaxpr/reduce_sum | solution.py:9
  92.9 0.0 copy-start
  92.9 3.6 %fusion.11 = (f32[512,2048]{1,0:T(8,128)S(1)}, f32[512,2048]{1,0:T(8,128)S(1)}) fusion(f32[512,2048]{1,0:T(8,128)S(1)} %get-tuple-element.179, f32[512,2048]{1,0:T(8,128)S(1)} %get-tuple-element.180), kind=kLoop, calls=%fused_computation.11.clone.1 | loop fusion | flops 19922944 | bytes 16777216 | tf_op jit(solution)/shard_map/while/body/eval_jaxpr/jit(_where)/select_n | solution.py:16
  96.5 0.0 copy-done
  96.5 2.3 %fusion.12 = f32[3,512]{1,0:T(4,128)S(1)} fusion(f32[512,2048]{1,0:T(8,128)S(1)} %get-tuple-element.181, f32[3,2048]{1,0:T(4,128)S(1)} %get-tuple-element.178, f32[512,2048]{1,0:T(8,128)S(1)} %get-tuple-element.182, f32[3,2048]{1,0:T(4,128)S(1)} %get-tuple-element.177, f32[3,512]{1,0:T(4,128)S(1)} %copy-done), kind=kLoop, calls=%fused_computation.6.clone.1 | loop fusion | flops 15727104 | bytes 8450048 | tf_op jit(solution)/shard_map/while/body/eval_jaxpr/reduce_sum | solution.py:23
  98.8 0.0 copy-done.1
  98.8 0.6 multiply_reduce_fusion.1
  99.4 31.7 %all-reduce = (f32[]{:T(128)}, f32[]{:T(128)}) all-reduce(f32[]{:T(128)} %get-tuple-element.119, f32[]{:T(128)} %get-tuple-element.118), channel_id=1, replica_groups=mesh['real'=2,'tile'=16] {'tile'}, use_global_device_ids=true, to_apply=%region_1.0 | all-reduce | flops 2 | bytes 16 | tf_op jit(solution)/shard_map/psum | solution.py:31
  132.5 0.6 multiply_reduce_fusion
  133.1 0.0 copy-start.2
  133.1 30.1 %psum.23 = f32[]{:T(128)} all-reduce(f32[]{:T(128)} %get-tuple-element.132), channel_id=1, replica_groups=mesh['real'=2,'tile'=16] {'tile'}, use_global_device_ids=true, to_apply=%region_10.11 | all-reduce | flops 1 | bytes 8 | tf_op jit(solution)/shard_map/psum | solution.py:50
  164.5 0.0 copy-done.3
  164.5 0.6 multiply_add_fusion
  165.1 0.0 copy-done.2
  (9 shorter events, 0.1 us)
Async XLA Ops:
  42.4 56.5 %copy-start.1 = (f32[3,512]{1,0:T(4,128)S(1)}, f32[3,512]{1,0:T(4,128)}, u32[]{:S(2)}) copy-start(f32[3,512]{1,0:T(4,128)} %param.6) | copy-start | bytes 18436
  42.4 122.2 %copy-start.3 = (f32[3,512]{1,0:T(4,128)S(1)}, f32[3,512]{1,0:T(4,128)}, u32[]{:S(2)}) copy-start(f32[3,512]{1,0:T(4,128)} %param.7) | copy-start | bytes 18436
  50.6 3.6 %copy-start = (f32[3,512]{1,0:T(4,128)S(1)}, f32[3,512]{1,0:T(4,128)}, u32[]{:S(2)}) copy-start(f32[3,512]{1,0:T(4,128)} %get-tuple-element.203) | copy-start | bytes 18436 | tf_op jit(solution)/shard_map/while
  64.7 3.6 %copy-start = (f32[3,512]{1,0:T(4,128)S(1)}, f32[3,512]{1,0:T(4,128)}, u32[]{:S(2)}) copy-start(f32[3,512]{1,0:T(4,128)} %get-tuple-element.203) | copy-start | bytes 18436 | tf_op jit(solution)/shard_map/while
  78.8 3.6 %copy-start = (f32[3,512]{1,0:T(4,128)S(1)}, f32[3,512]{1,0:T(4,128)}, u32[]{:S(2)}) copy-start(f32[3,512]{1,0:T(4,128)} %get-tuple-element.203) | copy-start | bytes 18436 | tf_op jit(solution)/shard_map/while
  92.9 3.6 %copy-start = (f32[3,512]{1,0:T(4,128)S(1)}, f32[3,512]{1,0:T(4,128)}, u32[]{:S(2)}) copy-start(f32[3,512]{1,0:T(4,128)} %get-tuple-element.203) | copy-start | bytes 18436 | tf_op jit(solution)/shard_map/while
  133.1 32.1 %copy-start.2 = (f32[3,512]{1,0:T(4,128)}, f32[3,512]{1,0:T(4,128)S(1)}, u32[]{:S(2)}) copy-start(f32[3,512]{1,0:T(4,128)S(1)} %get-tuple-element.133) | copy-start | bytes 18436
where the time goes:
time: 166 us; the launch traced here: 165 us
  blocking collectives  104 us (63%)
  other arithmetic  57.9 us (35%)
  between operations  3.34 us (2%)
    reduce_sum x4, other arithmetic, pair_terms(): squared = jnp.sum(separation * separation, axis=0)  32.7 us
    psum x1, blocking collectives, shards(): old_norm = lax.psum(jnp.sum(residual * residual), 'tile')  31.7 us
    psum x1, blocking collectives, shards(): new_norm = lax.psum(jnp.sum(new_residual * new_residual), 'tile')  30.1 us
    all_gather x1, blocking collectives, shards(): col_pos = lax.all_gather(positions, 'tile', axis=1, tiled=True)  23.7 us
    all_gather x1, blocking collectives, shards(): col_forces = lax.all_gather(residual, 'tile', axis=1, tiled=True)  18 us
    select_n x4, other arithmetic, pair_terms(): scalar_part = jnp.where(touching, 1.0 - 9.0 / 32.0 * radius, far_scalar)  14.3 us
    reduce_sum x4, other arithmetic, toward_rows(): jnp.sum(scalar_part[None] * col_forces[:, None, :] + (tensor_part * proje...  9.06 us

commit v1 on v0

--- a/solution.py
+++ b/solution.py
@@ -30,7 +30,7 @@
     own_blobs = positions.shape[1]
     old_norm = lax.psum(jnp.sum(residual * residual), "tile")
     col_pos = lax.all_gather(positions, "tile", axis=1, tiled=True)
-    col_forces = lax.all_gather(residual, "tile", axis=1, tiled=True)
+    col_forces = jnp.concatenate(lax.all_gather(residual, "tile"), axis=1)
     portion_cols = col_pos.shape[1]
     col_block = portion_cols
     for factor in (4, 2, 1):

time: 166 us -> 166 us (level)
  no operation moved by 1% of the time
where the time goes in v1:
time: 166 us; the launch traced here: 165 us
  blocking collectives  104 us (63%)
  other arithmetic  57.9 us (35%)
  between operations  3.34 us (2%)
    reduce_sum x4, other arithmetic, pair_terms(): squared = jnp.sum(separation * separation, axis=0)  32.7 us
    psum x1, blocking collectives, shards(): old_norm = lax.psum(jnp.sum(residual * residual), 'tile')  31.7 us
    psum x1, blocking collectives, shards(): new_norm = lax.psum(jnp.sum(new_residual * new_residual), 'tile')  30.1 us
    all_gather x1, blocking collectives, shards(): col_pos = lax.all_gather(positions, 'tile', axis=1, tiled=True)  23.7 us
    all_gather x1, blocking collectives, shards(): col_forces = jnp.concatenate(lax.all_gather(residual, 'tile'), axis=1)  18 us
    select_n x4, other arithmetic, pair_terms(): scalar_part = jnp.where(touching, 1.0 - 9.0 / 32.0 * radius, far_scalar)  14.3 us
    reduce_sum x4, other arithmetic, toward_rows(): jnp.sum(scalar_part[None] * col_forces[:, None, :] + (tensor_part * proje...  9.06 us

profile of v1, /device:TPU:0, one launch (start us, length us, event | category | flops | bytes accessed | tf_op | source)
XLA Modules:
  0.0 165.1 jit_solution(10569585680606642884)
XLA Ops:
  0.6 23.7 %all_gather.9 = f32[3,8192]{1,0:T(4,128)S(1)} all-gather(f32[3,512]{1,0:T(4,128)} %param.5), channel_id=1, replica_groups=mesh['real'=2,'tile'=16] {'tile'}, dimensions={1}, use_global_device_ids=true | all-gather | bytes 104448 | tf_op jit(solution)/shard_map/all_gather | solution.py:32
  24.3 18.0 %all-gather.1 = f32[16,3,512]{2,1,0:T(4,128)S(1)} all-gather(f32[1,3,512]{2,1,0:T(4,128)} %bitcast.5), channel_id=2, replica_groups=mesh['real'=2,'tile'=16] {'tile'}, dimensions={0}, use_global_device_ids=true | all-gather | bytes 104448 | tf_op jit(solution)/shard_map/all_gather | solution.py:33
  42.4 0.0 copy-start.1
  42.4 0.0 copy-start.3
  42.4 56.4 %while.14 = (s32[]{:T(128)}, f32[3,512]{1,0:T(4,128)S(1)}, f32[3,512]{1,0:T(4,128)}, f32[3,8192]{1,0:T(4,128)S(1)}, f32[3,8192]{1,0:T(4,128)S(1)}, /*index=5*/s32[]{:T(128)}, s32[]{:T(128)}, s32[]{:T(128)}, s32[]{:T(128)}) while((s32[]{:T(128)}, f32[3,512]{1,0:T(4,128)S(1)}, f32[3,512]{1,0:T(4,128)}, f32[3,8192]{1,0:T(4,128)S(1)}, ...), condition=%wide.region_6.7_spmd.clone, body=%wide.region_2.6_spmd.clone.sunk | while | flops 49284612 | bytes 33812656 | solution.py:46
  42.4 8.2 %fusion.10 = (f32[512,2048]{1,0:T(8,128)S(1)}, f32[512,2048]{1,0:T(8,128)S(1)}) fusion(f32[3,2048]{1,0:T(4,128)S(1)} %get-tuple-element.177, f32[3,512]{1,0:T(4,128)} %get-tuple-element.203, f32[3,2048]{1,0:T(4,128)S(1)} %get-tuple-element.178), kind=kLoop, calls=%fused_computation.3.clone.1 | loop fusion | flops 13631488 | bytes 8443904 | tf_op jit(solution)/shard_map/while/body/eval_jaxpr/reduce_sum | solution.py:9
  50.6 0.0 copy-start
  50.6 3.6 %fusion.11 = (f32[512,2048]{1,0:T(8,128)S(1)}, f32[512,2048]{1,0:T(8,128)S(1)}) fusion(f32[512,2048]{1,0:T(8,128)S(1)} %get-tuple-element.179, f32[512,2048]{1,0:T(8,128)S(1)} %get-tuple-element.180), kind=kLoop, calls=%fused_computation.11.clone.1 | loop fusion | flops 19922944 | bytes 16777216 | tf_op jit(solution)/shard_map/while/body/eval_jaxpr/jit(_where)/select_n | solution.py:16
  54.2 0.0 copy-done
  54.2 2.3 %fusion.12 = f32[3,512]{1,0:T(4,128)S(1)} fusion(f32[512,2048]{1,0:T(8,128)S(1)} %get-tuple-element.181, f32[3,2048]{1,0:T(4,128)S(1)} %get-tuple-element.178, f32[512,2048]{1,0:T(8,128)S(1)} %get-tuple-element.182, f32[3,2048]{1,0:T(4,128)S(1)} %get-tuple-element.177, f32[3,512]{1,0:T(4,128)S(1)} %copy-done), kind=kLoop, calls=%fused_computation.6.clone.1 | loop fusion | flops 15727104 | bytes 8450048 | tf_op jit(solution)/shard_map/while/body/eval_jaxpr/reduce_sum | solution.py:23
  56.5 8.2 %fusion.10 = (f32[512,2048]{1,0:T(8,128)S(1)}, f32[512,2048]{1,0:T(8,128)S(1)}) fusion(f32[3,2048]{1,0:T(4,128)S(1)} %get-tuple-element.177, f32[3,512]{1,0:T(4,128)} %get-tuple-element.203, f32[3,2048]{1,0:T(4,128)S(1)} %get-tuple-element.178), kind=kLoop, calls=%fused_computation.3.clone.1 | loop fusion | flops 13631488 | bytes 8443904 | tf_op jit(solution)/shard_map/while/body/eval_jaxpr/reduce_sum | solution.py:9
  64.7 0.0 copy-start
  64.7 3.6 %fusion.11 = (f32[512,2048]{1,0:T(8,128)S(1)}, f32[512,2048]{1,0:T(8,128)S(1)}) fusion(f32[512,2048]{1,0:T(8,128)S(1)} %get-tuple-element.179, f32[512,2048]{1,0:T(8,128)S(1)} %get-tuple-element.180), kind=kLoop, calls=%fused_computation.11.clone.1 | loop fusion | flops 19922944 | bytes 16777216 | tf_op jit(solution)/shard_map/while/body/eval_jaxpr/jit(_where)/select_n | solution.py:16
  68.3 0.0 copy-done
  68.3 2.3 %fusion.12 = f32[3,512]{1,0:T(4,128)S(1)} fusion(f32[512,2048]{1,0:T(8,128)S(1)} %get-tuple-element.181, f32[3,2048]{1,0:T(4,128)S(1)} %get-tuple-element.178, f32[512,2048]{1,0:T(8,128)S(1)} %get-tuple-element.182, f32[3,2048]{1,0:T(4,128)S(1)} %get-tuple-element.177, f32[3,512]{1,0:T(4,128)S(1)} %copy-done), kind=kLoop, calls=%fused_computation.6.clone.1 | loop fusion | flops 15727104 | bytes 8450048 | tf_op jit(solution)/shard_map/while/body/eval_jaxpr/reduce_sum | solution.py:23
  70.6 8.2 %fusion.10 = (f32[512,2048]{1,0:T(8,128)S(1)}, f32[512,2048]{1,0:T(8,128)S(1)}) fusion(f32[3,2048]{1,0:T(4,128)S(1)} %get-tuple-element.177, f32[3,512]{1,0:T(4,128)} %get-tuple-element.203, f32[3,2048]{1,0:T(4,128)S(1)} %get-tuple-element.178), kind=kLoop, calls=%fused_computation.3.clone.1 | loop fusion | flops 13631488 | bytes 8443904 | tf_op jit(solution)/shard_map/while/body/eval_jaxpr/reduce_sum | solution.py:9
  78.8 0.0 copy-start
  78.8 3.6 %fusion.11 = (f32[512,2048]{1,0:T(8,128)S(1)}, f32[512,2048]{1,0:T(8,128)S(1)}) fusion(f32[512,2048]{1,0:T(8,128)S(1)} %get-tuple-element.179, f32[512,2048]{1,0:T(8,128)S(1)} %get-tuple-element.180), kind=kLoop, calls=%fused_computation.11.clone.1 | loop fusion | flops 19922944 | bytes 16777216 | tf_op jit(solution)/shard_map/while/body/eval_jaxpr/jit(_where)/select_n | solution.py:16
  82.4 0.0 copy-done
  82.4 2.3 %fusion.12 = f32[3,512]{1,0:T(4,128)S(1)} fusion(f32[512,2048]{1,0:T(8,128)S(1)} %get-tuple-element.181, f32[3,2048]{1,0:T(4,128)S(1)} %get-tuple-element.178, f32[512,2048]{1,0:T(8,128)S(1)} %get-tuple-element.182, f32[3,2048]{1,0:T(4,128)S(1)} %get-tuple-element.177, f32[3,512]{1,0:T(4,128)S(1)} %copy-done), kind=kLoop, calls=%fused_computation.6.clone.1 | loop fusion | flops 15727104 | bytes 8450048 | tf_op jit(solution)/shard_map/while/body/eval_jaxpr/reduce_sum | solution.py:23
  84.7 8.2 %fusion.10 = (f32[512,2048]{1,0:T(8,128)S(1)}, f32[512,2048]{1,0:T(8,128)S(1)}) fusion(f32[3,2048]{1,0:T(4,128)S(1)} %get-tuple-element.177, f32[3,512]{1,0:T(4,128)} %get-tuple-element.203, f32[3,2048]{1,0:T(4,128)S(1)} %get-tuple-element.178), kind=kLoop, calls=%fused_computation.3.clone.1 | loop fusion | flops 13631488 | bytes 8443904 | tf_op jit(solution)/shard_map/while/body/eval_jaxpr/reduce_sum | solution.py:9
  92.9 0.0 copy-start
  92.9 3.6 %fusion.11 = (f32[512,2048]{1,0:T(8,128)S(1)}, f32[512,2048]{1,0:T(8,128)S(1)}) fusion(f32[512,2048]{1,0:T(8,128)S(1)} %get-tuple-element.179, f32[512,2048]{1,0:T(8,128)S(1)} %get-tuple-element.180), kind=kLoop, calls=%fused_computation.11.clone.1 | loop fusion | flops 19922944 | bytes 16777216 | tf_op jit(solution)/shard_map/while/body/eval_jaxpr/jit(_where)/select_n | solution.py:16
  96.5 0.0 copy-done
  96.5 2.3 %fusion.12 = f32[3,512]{1,0:T(4,128)S(1)} fusion(f32[512,2048]{1,0:T(8,128)S(1)} %get-tuple-element.181, f32[3,2048]{1,0:T(4,128)S(1)} %get-tuple-element.178, f32[512,2048]{1,0:T(8,128)S(1)} %get-tuple-element.182, f32[3,2048]{1,0:T(4,128)S(1)} %get-tuple-element.177, f32[3,512]{1,0:T(4,128)S(1)} %copy-done), kind=kLoop, calls=%fused_computation.6.clone.1 | loop fusion | flops 15727104 | bytes 8450048 | tf_op jit(solution)/shard_map/while/body/eval_jaxpr/reduce_sum | solution.py:23
  98.8 0.0 copy-done.1
  98.8 0.6 multiply_reduce_fusion.1
  99.4 31.7 %all-reduce = (f32[]{:T(128)}, f32[]{:T(128)}) all-reduce(f32[]{:T(128)} %get-tuple-element.119, f32[]{:T(128)} %get-tuple-element.118), channel_id=1, replica_groups=mesh['real'=2,'tile'=16] {'tile'}, use_global_device_ids=true, to_apply=%region_1.0 | all-reduce | flops 2 | bytes 16 | tf_op jit(solution)/shard_map/psum | solution.py:31
  132.5 0.6 multiply_reduce_fusion
  133.1 0.0 copy-start.2
  133.1 30.1 %psum.23 = f32[]{:T(128)} all-reduce(f32[]{:T(128)} %get-tuple-element.132), channel_id=1, replica_groups=mesh['real'=2,'tile'=16] {'tile'}, use_global_device_ids=true, to_apply=%region_10.11 | all-reduce | flops 1 | bytes 8 | tf_op jit(solution)/shard_map/psum | solution.py:50
  164.5 0.0 copy-done.3
  164.5 0.6 multiply_add_fusion
  165.1 0.0 copy-done.2
  (9 shorter events, 0.1 us)
Async XLA Ops:
  42.4 56.5 %copy-start.1 = (f32[3,512]{1,0:T(4,128)S(1)}, f32[3,512]{1,0:T(4,128)}, u32[]{:S(2)}) copy-start(f32[3,512]{1,0:T(4,128)} %param.6) | copy-start | bytes 18436
  42.4 122.2 %copy-start.3 = (f32[3,512]{1,0:T(4,128)S(1)}, f32[3,512]{1,0:T(4,128)}, u32[]{:S(2)}) copy-start(f32[3,512]{1,0:T(4,128)} %param.7) | copy-start | bytes 18436
  50.6 3.6 %copy-start = (f32[3,512]{1,0:T(4,128)S(1)}, f32[3,512]{1,0:T(4,128)}, u32[]{:S(2)}) copy-start(f32[3,512]{1,0:T(4,128)} %get-tuple-element.203) | copy-start | bytes 18436 | tf_op jit(solution)/shard_map/while
  64.7 3.6 %copy-start = (f32[3,512]{1,0:T(4,128)S(1)}, f32[3,512]{1,0:T(4,128)}, u32[]{:S(2)}) copy-start(f32[3,512]{1,0:T(4,128)} %get-tuple-element.203) | copy-start | bytes 18436 | tf_op jit(solution)/shard_map/while
  78.8 3.6 %copy-start = (f32[3,512]{1,0:T(4,128)S(1)}, f32[3,512]{1,0:T(4,128)}, u32[]{:S(2)}) copy-start(f32[3,512]{1,0:T(4,128)} %get-tuple-element.203) | copy-start | bytes 18436 | tf_op jit(solution)/shard_map/while
  92.9 3.6 %copy-start = (f32[3,512]{1,0:T(4,128)S(1)}, f32[3,512]{1,0:T(4,128)}, u32[]{:S(2)}) copy-start(f32[3,512]{1,0:T(4,128)} %get-tuple-element.203) | copy-start | bytes 18436 | tf_op jit(solution)/shard_map/while
  133.1 32.1 %copy-start.2 = (f32[3,512]{1,0:T(4,128)}, f32[3,512]{1,0:T(4,128)S(1)}, u32[]{:S(2)}) copy-start(f32[3,512]{1,0:T(4,128)S(1)} %get-tuple-element.133) | copy-start | bytes 18436
